TPU v7x, 256 devices: a whole 4x4x8 slice. The times are simulated.
256 devices in a mesh: grp: 8 (over y, core), row: 32 (over z, x).
Axes of the slice: x: 4, y: 4, z: 8, core: 2. Of those that a mesh axis runs over, the one named last changes fastest.
Arguments:
- fine_cols: int32 [10240, 5], P(('grp', 'row')), may hold values from 0 to 10239, as said below
- fine_blocks: bfloat16 [10240, 5, 128, 128], P(('grp', 'row'))
- prolong_cols: int32 [10240, 2], replicated, may hold values from 0 to 1023, as said below
- prolong_blocks: bfloat16 [10240, 2, 128, 128], P(('grp', 'row')), may hold values from -0.125 to 0.125
- agg_owner: int32 [1024], replicated, may hold values from 0 to 7, as said below
- coarse_rhs: float32 [1024, 128], P(('grp', 'row')), may hold values from -6 to 6
- lam_low: float32 [1], replicated, may hold values from 0.05 to 0.5
- lam_high: float32 [1], replicated, may hold values from 1.5 to 3.5
Outputs:
- coarse_operator: float32 [2048, 7, 128, 128], P(('grp', 'row'))
- coarse_solution: float32 [2048, 128], P(('grp', 'row'))
- coarse_residual: float32 [2048, 128], P(('grp', 'row'))
Inputs may be any that keep to these rules, and one draw needn't show every extreme that they name: fine_cols[i, 0] = i; the other 4 entries of row i are distinct rows (i + t) mod 10240 with 1 <= |t| <= 10; some row reaches |t| = 10. `prolong_cols`: the two entries of fine row i are two distinct ones of i // 10 - 1, i // 10, i // 10 + 1 in rising order, taken modulo 1024. `agg_owner`: the 4 aggregates made on one device go to distinct groups; for every row index some group owns one aggregate from each of the 8 groups at that row index.
All inputs are finite; a program needn't handle non-finite values.
Results may differ from a plain program's by a relative error of at most 0.0019.
Values may be sent and summed in bfloat16 or wider, within the bound.
A program may use at most 128 MiB of HBM per device.

v0:
```python
import jax
import jax.numpy as jnp
from jax import lax
from jax.sharding import PartitionSpec as P

HIGH = lax.Precision.HIGHEST


def extended_2(block, sides, width):
    for axis, dim in sides:
        count = lax.axis_size(axis)
        forward = [(i, i + 1) for i in range(count - 1)]
        forward.append((count - 1, 0))
        backward = [(target, source) for source, target in forward]
        low = lax.ppermute(
            lax.slice_in_dim(block, block.shape[dim] - width, None, axis=dim), axis, forward
        )
        high = lax.ppermute(lax.slice_in_dim(block, 0, width, axis=dim), axis, backward)
        block = jnp.concatenate([low, block, high], axis=dim)
    return block


def chebyshev_terms(lam_low, lam_high):
    center = 0.5 * (lam_high[0] + lam_low[0])
    radius = 0.5 * (lam_high[0] - lam_low[0])
    sigma_ratio = center / radius
    first_rho = 1.0 / sigma_ratio
    second_rho = 1.0 / (2.0 * sigma_ratio - first_rho)
    return (center, second_rho * first_rho, 2.0 * second_rho / radius)


def per_device(
    fine_cols, fine_blocks, prolong_cols, prolong_blocks, agg_owner, coarse_rhs, lam_low, lam_high
):
    rows_dev = fine_blocks.shape[0]
    band_width = fine_blocks.shape[2]
    groups = lax.axis_size("grp")
    rows_axis = lax.axis_size("row")
    devices = groups * rows_axis
    aggs_dev = coarse_rhs.shape[0]
    agg_rows = rows_dev // aggs_dev
    fine_total = rows_dev * devices
    coarse_total = aggs_dev * devices
    my_grp = lax.axis_index("grp")
    my_row = lax.axis_index("row")
    device = my_grp * rows_axis + my_row
    first_row = device * rows_dev
    offsets = jnp.arange(-2, 3, dtype=jnp.int32)
    group_ids = jnp.arange(groups, dtype=jnp.int32)
    p_pad = extended_2(prolong_blocks, ((("grp", "row"), 0),), agg_rows)
    pad_ids = (
        first_row - agg_rows + jnp.arange(rows_dev + 2 * agg_rows, dtype=jnp.int32)
    ) % fine_total
    cols_pad = jnp.take(prolong_cols, pad_ids, axis=0)

    def one_aggregate(agg_index):
        start = agg_index * agg_rows
        block_a = lax.dynamic_slice_in_dim(fine_blocks, start, agg_rows, 0)
        cols_here = lax.dynamic_slice_in_dim(fine_cols, start, agg_rows, 0)
        local_rows = start + jnp.arange(agg_rows, dtype=jnp.int32)
        global_rows = first_row + local_rows
        reach = (cols_here - global_rows[:, None] + agg_rows) % fine_total - agg_rows
        positions = local_rows[:, None] + agg_rows + reach
        p_near = jnp.take(p_pad, positions, axis=0)
        near_cols = jnp.take(cols_pad, positions, axis=0)
        agg_id = device * aggs_dev + agg_index
        shifted = (near_cols - agg_id + 2) % coarse_total - 2
        chosen = (shifted[..., None] == offsets).astype(jnp.float32)
        products = jnp.einsum(
            "iakm,iaqmn->iaqkn", block_a, p_near, preferred_element_type=jnp.float32
        )
        merged = jnp.einsum("iaqo,iaqkn->iokn", chosen, products, precision=HIGH).astype(
            jnp.bfloat16
        )
        own_blocks = lax.dynamic_slice_in_dim(prolong_blocks, start, agg_rows, 0)
        own_cols = lax.dynamic_slice_in_dim(cols_pad, start + agg_rows, agg_rows, 0)
        step_off = (own_cols - agg_id + 1) % coarse_total - 1
        term_blocks = jnp.einsum(
            "ipmk,iomn->ipokn", own_blocks, merged, preferred_element_type=jnp.float32
        )
        lifted = step_off[:, :, None, None, None]
        placing = (
            (lifted + 1 == jnp.arange(3, dtype=jnp.int32)[:, None])
            & (offsets[None, None, :, None, None] - lifted + 3 == jnp.arange(7, dtype=jnp.int32))
        ).astype(jnp.float32)
        return jnp.einsum("ipots,ipokn->tskn", placing, term_blocks, precision=HIGH)

    pieces = lax.map(one_aggregate, jnp.arange(aggs_dev, dtype=jnp.int32))
    partial_value = jnp.zeros((aggs_dev + 2, 7, band_width, band_width), jnp.float32)
    for target in range(3):
        partial_value = partial_value.at[target : target + aggs_dev].add(pieces[:, target])
    owners_mine = lax.dynamic_slice_in_dim(agg_owner, device * aggs_dev, aggs_dev, 0)
    send_onehot = (owners_mine[:, None] == group_ids).astype(jnp.float32)
    send_rhs = jnp.einsum("kg,kn->gn", send_onehot, coarse_rhs, precision=HIGH)
    extended = extended_2(partial_value, ((("grp", "row"), 0),), 1)
    native = partial_value[1 : aggs_dev + 1]
    native = native.at[0].add(extended[0])
    native = native.at[aggs_dev - 1].add(extended[aggs_dev + 3])
    send_rows = jnp.einsum("kg,ksmn->gsmn", send_onehot, native, precision=HIGH)
    got_rows, got_rhs = (
        lax.all_to_all(send_rows, "grp", split_axis=0, concat_axis=0, tiled=True),
        lax.all_to_all(send_rhs, "grp", split_axis=0, concat_axis=0, tiled=True),
    )
    source_dev = group_ids * rows_axis + my_row
    agg_table = source_dev[:, None] * aggs_dev + jnp.arange(aggs_dev, dtype=jnp.int32)
    matches = (jnp.take(agg_owner, agg_table, axis=0) == my_grp).astype(jnp.int32)
    slot_agg = source_dev * aggs_dev + jnp.sum(
        matches * jnp.arange(aggs_dev, dtype=jnp.int32), axis=1
    )
    near_ids = (slot_agg[:, None] + jnp.arange(7, dtype=jnp.int32) - 3) % coarse_total
    near_dev = near_ids // aggs_dev
    near_grp = near_dev // rows_axis
    near_row = near_dev % rows_axis
    near_owner = jnp.take(agg_owner, near_ids, axis=0)

    def operate(vector):
        whole = lax.all_gather(vector, ("grp", "row"), axis=0, tiled=True)
        nearby = jnp.take(whole, (near_owner * rows_axis + near_row) * groups + near_grp, axis=0)
        return jnp.einsum("gsmn,gsn->gm", got_rows, nearby, precision=HIGH)

    center, old_weight, resid_weight = chebyshev_terms(lam_low, lam_high)
    first_iter = got_rhs / center
    first_resid = got_rhs - operate(first_iter)
    second_iter = first_iter + old_weight * first_iter + resid_weight * first_resid
    second_resid = got_rhs - operate(second_iter)
    return (got_rows, second_iter, second_resid)


def solution(mesh):
    return jax.shard_map(
        per_device,
        mesh=mesh,
        in_specs=(
            P(("grp", "row"), None),
            P(("grp", "row"), None, None, None),
            P(),
            P(("grp", "row"), None, None, None),
            P(),
            P(("grp", "row"), None),
            P(),
            P(),
        ),
        out_specs=(
            P(("grp", "row"), None, None, None),
            P(("grp", "row"), None),
            P(("grp", "row"), None),
        ),
        check_vma=False,
    )
```

profile of v0, /device:TPU:1, one launch (start us, length us, event | category | flops | bytes accessed | tf_op | source)
XLA Modules:
  0.0 583.9 jit_solution(10987784176769533986)
XLA Ops:
  11.5 7.1 %collective-permute-start.1 = (bf16[10,2,128,128]{3,2,1,0:T(8,128)(2,1)S(1)}, bf16[10,2,128,128]{3,2,1,0:T(8,128)(2,1)}, u32[]{:S(2)}, u32[]{:S(2)}) collective-permute-start(bf16[10,2,128,128]{3,2,1,0:T(8,128)(2,1)S(1)} %get-tuple-element.460), channel_id=1, source_target_pairs={{1,0},{2,1},{3,2},{4,3},{5,4},{6,5},{7,6},{8,7},{9,8},{10,9},{11,1... | collective-permute-start | bytes 1966088 | tf_op jit(solution)/shard_map/ppermute | solution.py:18
  18.6 3.9 copy.53
  22.5 3.1 gather_fusion.2
  25.8 7.8 %collective-permute-done = bf16[10,2,128,128]{3,2,1,0:T(8,128)(2,1)} collective-permute-done((bf16[10,2,128,128]{3,2,1,0:T(8,128)(2,1)}, bf16[10,2,128,128]{3,2,1,0:T(8,128)(2,1)}, u32[]{:S(2)}, u32[]{:S(2)}) %collective-permute-start) | collective-permute-done | bytes 655392 | tf_op jit(solution)/shard_map/ppermute | solution.py:15
  33.6 3.3 pad_maximum_fusion
  36.9 265.3 %while.22 = (s32[]{:T(128)}, f32[4,3,7,128,128]{4,2,3,1,0:T(8,128)}, s32[4]{0:T(128)S(1)}, s32[60,2]{0,1:T(2,128)S(1)}, s32[]{:T(128)}, /*index=5*/s32[40,5]{0,1...) while((s32[]{:T(128)}, ...), condition=%wide.region_1.2_spmd.clone.clone, body=%wide.region_0.1_spmd.clone.clone.sunk | while | flops 1352506368 | bytes 91372768 | solution.py:88
  38.7 4.9 gather_fusion
  43.6 4.3 copy.98
  47.8 5.2 fusion.101
  53.0 10.1 %copy.99 = f32[10,5,2,128,128]{4,1,2,3,0:T(8,128)} copy(f32[10,5,2,128,128]{3,4,2,1,0:T(8,128)} %fusion.101) | data formatting | bytes 13107200 | tf_op jit(solution)/shard_map/while/body/eval_jaxpr/iakm,iaqmn->iaqkn/transpose | solution.py:69
  64.8 10.6 %fusion.103 = bf16[10,5,128,128,1]{3,1,2,0,4:T(8,128)(2,1)S(1)} fusion(f32[10,5,2,128,128]{4,1,2,3,0:T(8,128)} %copy.99, s32[10,5,2]{1,2,0:T(2,128)S(1)} %copy.102, s32[5]{0:T(128)S(1)} %iota_add_fusion.3), kind=kOutput, calls=%fused_computation.16.clone.1 | convolution fusion | flops 99123696 | bytes 8192420 | tf_op jit(solution)/shard_map/while/body/eval_jaxpr/iaqo,iaqkn->iokn/dot_general | solution.py:72
  75.4 3.8 convolution_bitcast_fusion.2
  79.2 11.5 %copy.103 = f32[10,2,5,128,128]{4,0,1,2,3:T(8,128)} copy(f32[10,2,5,128,128]{3,4,1,2,0:T(8,128)} %convolution_bitcast_fusion.2) | data formatting | bytes 13107200 | tf_op jit(solution)/shard_map/while/body/eval_jaxpr/ipmk,iomn->ipokn/transpose | solution.py:78
  90.9 12.4 %bitcast_dynamic-update-slice_fusion.2 = f32[4,3,7,128,128]{4,2,3,1,0:T(8,128)} fusion(f32[4,3,7,128,128]{4,2,3,1,0:T(8,128)} %get-tuple-element.550, s32[]{:T(128)} %get-tuple-element.549, f32[10,2,5,128,128]{4,0,1,2,3:T(8,128)} %copy.103, pred[10,2,5,7]{0,3,1,2:T(8,128)(4,1)S(1)} %iota_compare_fusion.6, pred[10,2,3]{0,1,2:T(4,128)(4,1)S(1)} %iota_compare_fusion.7), kind=kOutput, calls=%fused_computation.21.clone.1 | convolution fusion | flops 412878912 | bytes 12059896 | tf_op jit(solution)/shard_map/while/body/eval_jaxpr/ipots,ipokn->tskn/dot_general | solution.py:86
  105.0 4.9 gather_fusion
  109.9 4.3 copy.98
  114.2 5.2 fusion.101
  119.4 10.1 %copy.99 = f32[10,5,2,128,128]{4,1,2,3,0:T(8,128)} copy(f32[10,5,2,128,128]{3,4,2,1,0:T(8,128)} %fusion.101) | data formatting | bytes 13107200 | tf_op jit(solution)/shard_map/while/body/eval_jaxpr/iakm,iaqmn->iaqkn/transpose | solution.py:69
  131.1 10.6 %fusion.103 = bf16[10,5,128,128,1]{3,1,2,0,4:T(8,128)(2,1)S(1)} fusion(f32[10,5,2,128,128]{4,1,2,3,0:T(8,128)} %copy.99, s32[10,5,2]{1,2,0:T(2,128)S(1)} %copy.102, s32[5]{0:T(128)S(1)} %iota_add_fusion.3), kind=kOutput, calls=%fused_computation.16.clone.1 | convolution fusion | flops 99123696 | bytes 8192420 | tf_op jit(solution)/shard_map/while/body/eval_jaxpr/iaqo,iaqkn->iokn/dot_general | solution.py:72
  141.8 3.8 convolution_bitcast_fusion.2
  145.5 11.5 %copy.103 = f32[10,2,5,128,128]{4,0,1,2,3:T(8,128)} copy(f32[10,2,5,128,128]{3,4,1,2,0:T(8,128)} %convolution_bitcast_fusion.2) | data formatting | bytes 13107200 | tf_op jit(solution)/shard_map/while/body/eval_jaxpr/ipmk,iomn->ipokn/transpose | solution.py:78
  157.2 12.4 %bitcast_dynamic-update-slice_fusion.2 = f32[4,3,7,128,128]{4,2,3,1,0:T(8,128)} fusion(f32[4,3,7,128,128]{4,2,3,1,0:T(8,128)} %get-tuple-element.550, s32[]{:T(128)} %get-tuple-element.549, f32[10,2,5,128,128]{4,0,1,2,3:T(8,128)} %copy.103, pred[10,2,5,7]{0,3,1,2:T(8,128)(4,1)S(1)} %iota_compare_fusion.6, pred[10,2,3]{0,1,2:T(4,128)(4,1)S(1)} %iota_compare_fusion.7), kind=kOutput, calls=%fused_computation.21.clone.1 | convolution fusion | flops 412878912 | bytes 12059896 | tf_op jit(solution)/shard_map/while/body/eval_jaxpr/ipots,ipokn->tskn/dot_general | solution.py:86
  171.3 4.9 gather_fusion
  176.2 4.3 copy.98
  180.5 5.2 fusion.101
  185.7 10.1 %copy.99 = f32[10,5,2,128,128]{4,1,2,3,0:T(8,128)} copy(f32[10,5,2,128,128]{3,4,2,1,0:T(8,128)} %fusion.101) | data formatting | bytes 13107200 | tf_op jit(solution)/shard_map/while/body/eval_jaxpr/iakm,iaqmn->iaqkn/transpose | solution.py:69
  197.4 10.6 %fusion.103 = bf16[10,5,128,128,1]{3,1,2,0,4:T(8,128)(2,1)S(1)} fusion(f32[10,5,2,128,128]{4,1,2,3,0:T(8,128)} %copy.99, s32[10,5,2]{1,2,0:T(2,128)S(1)} %copy.102, s32[5]{0:T(128)S(1)} %iota_add_fusion.3), kind=kOutput, calls=%fused_computation.16.clone.1 | convolution fusion | flops 99123696 | bytes 8192420 | tf_op jit(solution)/shard_map/while/body/eval_jaxpr/iaqo,iaqkn->iokn/dot_general | solution.py:72
  208.1 3.8 convolution_bitcast_fusion.2
  211.8 11.5 %copy.103 = f32[10,2,5,128,128]{4,0,1,2,3:T(8,128)} copy(f32[10,2,5,128,128]{3,4,1,2,0:T(8,128)} %convolution_bitcast_fusion.2) | data formatting | bytes 13107200 | tf_op jit(solution)/shard_map/while/body/eval_jaxpr/ipmk,iomn->ipokn/transpose | solution.py:78
  223.5 12.4 %bitcast_dynamic-update-slice_fusion.2 = f32[4,3,7,128,128]{4,2,3,1,0:T(8,128)} fusion(f32[4,3,7,128,128]{4,2,3,1,0:T(8,128)} %get-tuple-element.550, s32[]{:T(128)} %get-tuple-element.549, f32[10,2,5,128,128]{4,0,1,2,3:T(8,128)} %copy.103, pred[10,2,5,7]{0,3,1,2:T(8,128)(4,1)S(1)} %iota_compare_fusion.6, pred[10,2,3]{0,1,2:T(4,128)(4,1)S(1)} %iota_compare_fusion.7), kind=kOutput, calls=%fused_computation.21.clone.1 | convolution fusion | flops 412878912 | bytes 12059896 | tf_op jit(solution)/shard_map/while/body/eval_jaxpr/ipots,ipokn->tskn/dot_general | solution.py:86
  237.6 4.9 gather_fusion
  242.5 4.3 copy.98
  246.7 5.2 fusion.101
  252.0 10.1 %copy.99 = f32[10,5,2,128,128]{4,1,2,3,0:T(8,128)} copy(f32[10,5,2,128,128]{3,4,2,1,0:T(8,128)} %fusion.101) | data formatting | bytes 13107200 | tf_op jit(solution)/shard_map/while/body/eval_jaxpr/iakm,iaqmn->iaqkn/transpose | solution.py:69
  263.7 10.6 %fusion.103 = bf16[10,5,128,128,1]{3,1,2,0,4:T(8,128)(2,1)S(1)} fusion(f32[10,5,2,128,128]{4,1,2,3,0:T(8,128)} %copy.99, s32[10,5,2]{1,2,0:T(2,128)S(1)} %copy.102, s32[5]{0:T(128)S(1)} %iota_add_fusion.3), kind=kOutput, calls=%fused_computation.16.clone.1 | convolution fusion | flops 99123696 | bytes 8192420 | tf_op jit(solution)/shard_map/while/body/eval_jaxpr/iaqo,iaqkn->iokn/dot_general | solution.py:72
  274.3 3.8 convolution_bitcast_fusion.2
  278.1 11.5 %copy.103 = f32[10,2,5,128,128]{4,0,1,2,3:T(8,128)} copy(f32[10,2,5,128,128]{3,4,1,2,0:T(8,128)} %convolution_bitcast_fusion.2) | data formatting | bytes 13107200 | tf_op jit(solution)/shard_map/while/body/eval_jaxpr/ipmk,iomn->ipokn/transpose | solution.py:78
  289.8 12.4 %bitcast_dynamic-update-slice_fusion.2 = f32[4,3,7,128,128]{4,2,3,1,0:T(8,128)} fusion(f32[4,3,7,128,128]{4,2,3,1,0:T(8,128)} %get-tuple-element.550, s32[]{:T(128)} %get-tuple-element.549, f32[10,2,5,128,128]{4,0,1,2,3:T(8,128)} %copy.103, pred[10,2,5,7]{0,3,1,2:T(8,128)(4,1)S(1)} %iota_compare_fusion.6, pred[10,2,3]{0,1,2:T(4,128)(4,1)S(1)} %iota_compare_fusion.7), kind=kOutput, calls=%fused_computation.21.clone.1 | convolution fusion | flops 412878912 | bytes 12059896 | tf_op jit(solution)/shard_map/while/body/eval_jaxpr/ipots,ipokn->tskn/dot_general | solution.py:86
  306.8 17.2 %collective-permute-done.2 = f32[1,7,128,128]{3,1,2,0:T(8,128)S(1)} collective-permute-done((f32[1,7,128,128]{3,1,2,0:T(8,128)S(1)}, f32[1,7,128,128]{3,1,2,0:T(8,128)S(1)}, u32[]{:S(2)}, u32[]{:S(2)}) %collective-permute-start.2) | collective-permute-done | bytes 458784 | tf_op jit(solution)/shard_map/ppermute | solution.py:15
  325.2 6.8 %all-to-all-start.1 = ((f32[8,1,128]{2,1,0:T(1,128)}), f32[8,1,128]{2,1,0:T(1,128)S(1)}, u32[]{:S(2)}, u32[]{:S(2)}) async-start(f32[8,1,128]{2,1,0:T(1,128)} %bitcast.7), calls=%async_computation.1 | async-start | bytes 8192 | tf_op jit(solution)/shard_map/all_to_all | solution.py:102
  334.5 3.4 fusion.42
  337.9 2.5 copy.59
  340.4 9.1 %all-to-all-start = ((f32[8,7,128,128]{3,2,1,0:T(8,128)}), f32[8,7,128,128]{3,2,1,0:T(8,128)}, u32[]{:S(2)}, u32[]{:S(2)}) async-start(f32[8,7,128,128]{3,2,1,0:T(8,128)} %copy.59), calls=%async_computation | async-start | bytes 7340032 | tf_op jit(solution)/shard_map/all_to_all | solution.py:101
  354.2 101.2 %all-gather.3.cloned.1.call-done = f32[2048,128]{1,0:T(8,128)} async-done(((f32[8,128]{1,0:T(8,128)}), f32[2048,128]{1,0:T(8,128)}) %all-gather.3.cloned.1.call-update) | async-done | bytes 1048592 | tf_op jit(solution)/shard_map/all_gather | solution.py:117
  457.3 5.5 fusion.48
  463.5 101.2 %all-gather.5.cloned.1.call-done = f32[2048,128]{1,0:T(8,128)} async-done(((f32[8,128]{1,0:T(8,128)}), f32[2048,128]{1,0:T(8,128)}) %all-gather.5.cloned.1.call-update) | async-done | bytes 1048592 | tf_op jit(solution)/shard_map/all_gather | solution.py:117
  566.6 5.6 fusion.46
  572.8 4.3 copy.118
  (145 shorter events, 29.3 us)
Async XLA Ops:
  7.2 317.2 %copy-start = (f32[4,128]{1,0:T(4,128)S(1)}, f32[4,128]{1,0:T(4,128)}, u32[]{:S(2)}) copy-start(f32[4,128]{1,0:T(4,128)} %param.27) | copy-start | bytes 6148
  9.4 24.2 %copy-start.2 = (bf16[40,2,128,128]{3,2,1,0:T(8,128)(2,1)S(1)}, bf16[40,2,128,128]{3,2,1,0:T(8,128)(2,1)}, u32[]{:S(2)}) copy-start(bf16[40,2,128,128]{3,2,1,0:T(8,128)(2,1)} %param.25) | copy-start | bytes 7864324
  9.4 24.2 %collective-permute-start = (bf16[10,2,128,128]{3,2,1,0:T(8,128)(2,1)}, bf16[10,2,128,128]{3,2,1,0:T(8,128)(2,1)}, u32[]{:S(2)}, u32[]{:S(2)}) collective-permute-start(bf16[10,2,128,128]{3,2,1,0:T(8,128)(2,1)} %get-tuple-element.459), channel_id=1, source_target_pairs={{0,1},{1,2},{2,3},{3,4},{4,5},{5,6},{6,7},{7,8},{8,9},{9,10},{10,1... | collective-permute-start | bytes 1966088 | tf_op jit(solution)/shard_map/ppermute | solution.py:15
  11.5 22.2 %collective-permute-start.1 = (bf16[10,2,128,128]{3,2,1,0:T(8,128)(2,1)S(1)}, bf16[10,2,128,128]{3,2,1,0:T(8,128)(2,1)}, u32[]{:S(2)}, u32[]{:S(2)}) collective-permute-start(bf16[10,2,128,128]{3,2,1,0:T(8,128)(2,1)S(1)} %get-tuple-element.460), channel_id=1, source_target_pairs={{1,0},{2,1},{3,2},{4,3},{5,4},{6,5},{7,6},{8,7},{9,8},{10,9},{11,1... | collective-permute-start | bytes 1966088 | tf_op jit(solution)/shard_map/ppermute | solution.py:18
  25.8 11.1 %copy-start.5 = (s32[40,5]{0,1:T(8,128)S(1)}, s32[40,5]{0,1:T(8,128)}, u32[]{:S(2)}) copy-start(s32[40,5]{0,1:T(8,128)} %param.22) | copy-start | bytes 2404
  64.8 10.6 %copy-start.3 = (bf16[40,2,128,128]{3,2,1,0:T(8,128)(2,1)S(1)}, bf16[40,2,128,128]{3,2,1,0:T(8,128)(2,1)}, u32[]{:S(2)}) copy-start(bf16[40,2,128,128]{3,2,1,0:T(8,128)(2,1)} %get-tuple-element.602) | copy-start | bytes 7864324 | tf_op jit(solution)/shard_map/while
  131.1 10.6 %copy-start.3 = (bf16[40,2,128,128]{3,2,1,0:T(8,128)(2,1)S(1)}, bf16[40,2,128,128]{3,2,1,0:T(8,128)(2,1)}, u32[]{:S(2)}) copy-start(bf16[40,2,128,128]{3,2,1,0:T(8,128)(2,1)} %get-tuple-element.602) | copy-start | bytes 7864324 | tf_op jit(solution)/shard_map/while
  197.4 10.6 %copy-start.3 = (bf16[40,2,128,128]{3,2,1,0:T(8,128)(2,1)S(1)}, bf16[40,2,128,128]{3,2,1,0:T(8,128)(2,1)}, u32[]{:S(2)}) copy-start(bf16[40,2,128,128]{3,2,1,0:T(8,128)(2,1)} %get-tuple-element.602) | copy-start | bytes 7864324 | tf_op jit(solution)/shard_map/while
  263.7 10.6 %copy-start.3 = (bf16[40,2,128,128]{3,2,1,0:T(8,128)(2,1)S(1)}, bf16[40,2,128,128]{3,2,1,0:T(8,128)(2,1)}, u32[]{:S(2)}) copy-start(bf16[40,2,128,128]{3,2,1,0:T(8,128)(2,1)} %get-tuple-element.602) | copy-start | bytes 7864324 | tf_op jit(solution)/shard_map/while
  302.2 3.4 copy-start.4
  306.4 17.6 %collective-permute-start.2 = (f32[1,7,128,128]{3,1,2,0:T(8,128)S(1)}, f32[1,7,128,128]{3,1,2,0:T(8,128)S(1)}, u32[]{:S(2)}, u32[]{:S(2)}) collective-permute-start(f32[1,7,128,128]{3,1,2,0:T(8,128)S(1)} %slice.195), channel_id=1, source_target_pairs={{0,1},{1,2},{2,3},{3,4},{4,5},{5,6},{6,7},{7,8},{8,9},{9,10},{10,1... | collective-permute-start | bytes 1376264 | tf_op jit(solution)/shard_map/ppermute | solution.py:15
  306.6 17.7 %copy-start.1 = (s32[1024]{0:T(1024)S(1)}, s32[1024]{0:T(1024)}, u32[]{:S(2)}) copy-start(s32[1024]{0:T(1024)} %param.26) | copy-start | bytes 12292
  324.2 10.2 %collective-permute-start.3 = (f32[1,7,128,128]{3,1,2,0:T(8,128)S(1)}, f32[1,7,128,128]{3,1,2,0:T(8,128)S(1)}, u32[]{:S(2)}, u32[]{:S(2)}) collective-permute-start(f32[1,7,128,128]{3,1,2,0:T(8,128)S(1)} %get-tuple-element.457), channel_id=1, source_target_pairs={{1,0},{2,1},{3,2},{4,3},{5,4},{6,5},{7,6},{8,7},{9,8},{10,9},{11,1... | collective-permute-start | bytes 1376264 | tf_op jit(solution)/shard_map/ppermute | solution.py:18
  325.2 15.2 %all-to-all-start.1 = ((f32[8,1,128]{2,1,0:T(1,128)}), f32[8,1,128]{2,1,0:T(1,128)S(1)}, u32[]{:S(2)}, u32[]{:S(2)}) async-start(f32[8,1,128]{2,1,0:T(1,128)} %bitcast.7), calls=%async_computation.1 | async-start | bytes 8192 | tf_op jit(solution)/shard_map/all_to_all | solution.py:102
  340.4 117.0 %all-to-all-start = ((f32[8,7,128,128]{3,2,1,0:T(8,128)}), f32[8,7,128,128]{3,2,1,0:T(8,128)}, u32[]{:S(2)}, u32[]{:S(2)}) async-start(f32[8,7,128,128]{3,2,1,0:T(8,128)} %copy.59), calls=%async_computation | async-start | bytes 7340032 | tf_op jit(solution)/shard_map/all_to_all | solution.py:101
  349.5 106.0 %all-gather.3.cloned.1.call-start = ((), (), s32[]{:S(2)}) async-start(), calls=%async_computation.2 | async-start | bytes 1052672 | tf_op jit(solution)/shard_map/all_gather | solution.py:117
  351.4 213.3 %all-gather.5.cloned.1.call-start = ((), (), s32[]{:S(2)}) async-start(), calls=%async_computation.3 | async-start | bytes 1052672 | tf_op jit(solution)/shard_map/all_gather | solution.py:117
Sparse Core Ops, SparseCore 0:
  354.6 100.8 all-gather.2
  463.7 100.9 all-gather.4
where the time goes:
time: 587 us; the launch traced here: 584 us
  waiting for transfers between devices  230 us (39%)
  local copies, waits for them, and re-layouts  156 us (27%)
  matrix products  143 us (24%)
  starting transfers between devices  25.5 us (4%)
  between operations  15.7 us (3%)
  other arithmetic  8.03 us (1%)
  loops' own time  5.94 us (1%)
    all_gather x2, waiting for transfers between devices, operate(): whole = lax.all_gather(vector, ('grp', 'row'), axis=0, tiled=True)  202 us
    dot_general x4, matrix products, one_aggregate(): return jnp.einsum('ipots,ipokn->tskn', placing, term_blocks, precision=HIGH)  49.6 us
    transpose x4, local copies, waits for them, and re-layouts, one_aggregate(): jnp.einsum('ipmk,iomn->ipokn', own_blocks, merged, preferred_element_type...  45.9 us
    dot_general x4, matrix products, one_aggregate(): jnp.einsum('iaqo,iaqkn->iokn', chosen, products, precision=HIGH)  42.5 us
    transpose x4, local copies, waits for them, and re-layouts, one_aggregate(): jnp.einsum('iakm,iaqmn->iaqkn', block_a, p_near, preferred_element_type=j...  40.5 us
    gather x8, local copies, waits for them, and re-layouts, one_aggregate(): p_near = jnp.take(p_pad, positions, axis=0)  36.6 us
    ppermute x2, waiting for transfers between devices, extended_2(): lax.ppermute(lax.slice_in_dim(block, block.shape[dim] - width, None, axis...  25.1 us
    dot_general x4, matrix products, one_aggregate(): jnp.einsum('iakm,iaqmn->iaqkn', block_a, p_near, preferred_element_type=j...  20.8 us
  transfers between devices with their start and end apart: 8, of which 5 were waited for; matrix products, arithmetic and copies ran while one was open for 3% of the time, Pallas kernels for 0%

commit v1 on v0

--- a/solution.py
+++ b/solution.py
@@ -114,7 +114,15 @@
     near_owner = jnp.take(agg_owner, near_ids, axis=0)
 
     def operate(vector):
-        whole = lax.all_gather(vector, ("grp", "row"), axis=0, tiled=True)
+        whole = jnp.concatenate(
+            lax.all_to_all(
+                jnp.stack([vector for _ in range(lax.axis_size(("grp", "row")))]),
+                ("grp", "row"),
+                0,
+                0,
+            ),
+            0,
+        )
         nearby = jnp.take(whole, (near_owner * rows_axis + near_row) * groups + near_grp, axis=0)
         return jnp.einsum("gsmn,gsn->gm", got_rows, nearby, precision=HIGH)
 

time: 587 us -> 458 us (0.78)
  waiting for transfers between devices: 230 us -> 66.1 us
  blocking collectives: 0 us -> 39.3 us
  between operations: 15.7 us -> 2.36 us
  starting transfers between devices: 25.5 us -> 34.8 us
    all_gather x2 -> x0, waiting for transfers between devices: 202 us -> none  [operate(): whole = lax.all_gather(vector, ('grp', 'row'), axis=0, tiled=True)]
    all_to_all x0 -> x1, blocking collectives: none -> 39.3 us  [operate(): lax.all_to_all(jnp.stack([vector for _ in range(lax.axis_size(('grp', 'ro...]
    all_to_all x1, waiting for transfers between devices: 0.01 us -> 38.9 us  [per_device(): lax.all_to_all(send_rows, 'grp', split_axis=0, concat_axis=0, tiled=True)]
    all_to_all x0 -> x1, starting transfers between devices: none -> 9.69 us  [operate(): lax.all_to_all(jnp.stack([vector for _ in range(lax.axis_size(('grp', 'ro...]
    ppermute x2, waiting for transfers between devices: 25.1 us -> 17.3 us  [extended_2(): lax.ppermute(lax.slice_in_dim(block, block.shape[dim] - width, None, axis...]
    ppermute x2, waiting for transfers between devices: 2.4 us -> 9.9 us  [extended_2(): lax.ppermute(lax.slice_in_dim(block, 0, width, axis=dim), axis, backward)]
  transfers between devices with their start and end apart: 8 -> 7, of which waited for: 5 -> 3; matrix products, arithmetic and copies ran while one was open for 3% -> 63% of each run, Pallas kernels for 0% -> 0%
where the time goes in v1:
time: 458 us; the launch traced here: 455 us
  local copies, waits for them, and re-layouts  156 us (34%)
  matrix products  143 us (31%)
  waiting for transfers between devices  66.1 us (14%)
  blocking collectives  39.3 us (9%)
  starting transfers between devices  34.8 us (8%)
  other arithmetic  6.83 us (1%)
  loops' own time  6.1 us (1%)
    dot_general x4, matrix products, one_aggregate(): return jnp.einsum('ipots,ipokn->tskn', placing, term_blocks, precision=HIGH)  49.6 us
    transpose x4, local copies, waits for them, and re-layouts, one_aggregate(): jnp.einsum('ipmk,iomn->ipokn', own_blocks, merged, preferred_element_type...  45.9 us
    dot_general x4, matrix products, one_aggregate(): jnp.einsum('iaqo,iaqkn->iokn', chosen, products, precision=HIGH)  42.5 us
    transpose x4, local copies, waits for them, and re-layouts, one_aggregate(): jnp.einsum('iakm,iaqmn->iaqkn', block_a, p_near, preferred_element_type=j...  40.5 us
    all_to_all x1, blocking collectives, operate(): lax.all_to_all(jnp.stack([vector for _ in range(lax.axis_size(('grp', 'ro...  39.3 us
    all_to_all x1, waiting for transfers between devices, per_device(): lax.all_to_all(send_rows, 'grp', split_axis=0, concat_axis=0, tiled=True)  38.9 us
    gather x8, local copies, waits for them, and re-layouts, one_aggregate(): p_near = jnp.take(p_pad, positions, axis=0)  36.6 us
    dot_general x4, matrix products, one_aggregate(): jnp.einsum('iakm,iaqmn->iaqkn', block_a, p_near, preferred_element_type=j...  20.8 us
  transfers between devices with their start and end apart: 7, of which 3 were waited for; matrix products, arithmetic and copies ran while one was open for 63% of the time, Pallas kernels for 0%

profile of v1, /device:TPU:1, one launch (start us, length us, event | category | flops | bytes accessed | tf_op | source)
XLA Modules:
  0.0 455.1 jit_solution(12432597916977112288)
XLA Ops:
  4.9 7.1 %collective-permute-start.1 = (bf16[10,2,128,128]{3,2,1,0:T(8,128)(2,1)S(1)}, bf16[10,2,128,128]{3,2,1,0:T(8,128)(2,1)}, u32[]{:S(2)}, u32[]{:S(2)}) collective-permute-start(bf16[10,2,128,128]{3,2,1,0:T(8,128)(2,1)S(1)} %get-tuple-element.460), channel_id=1, source_target_pairs={{1,0},{2,1},{3,2},{4,3},{5,4},{6,5},{7,6},{8,7},{9,8},{10,9},{11,1... | collective-permute-start | bytes 1966088 | tf_op jit(solution)/shard_map/ppermute | solution.py:18
  13.7 5.5 %all-to-all-start.1 = ((f32[8,1,128]{2,1,0:T(1,128)}), f32[8,1,128]{2,1,0:T(1,128)S(1)}, u32[]{:S(2)}, u32[]{:S(2)}) async-start(f32[8,1,128]{2,1,0:T(1,128)} %bitcast.7), calls=%async_computation.1 | async-start | bytes 8192 | tf_op jit(solution)/shard_map/all_to_all | solution.py:102
  19.2 4.1 copy.53
  23.3 3.1 gather_fusion.2
  28.9 9.7 %all-to-all-start.2 = ((f32[256,8,128]{2,1,0:T(8,128)}), f32[256,8,128]{2,1,0:T(8,128)}, u32[]{:S(2)}, u32[]{:S(2)}) async-start(f32[256,8,128]{2,1,0:T(8,128)} %stack.4), calls=%async_computation.2 | async-start | bytes 2097152 | tf_op jit(solution)/shard_map/all_to_all | solution.py:118
  38.7 3.3 pad_maximum_fusion
  42.0 265.4 %while.22 = (s32[]{:T(128)}, f32[4,3,7,128,128]{4,2,3,1,0:T(8,128)}, s32[4]{0:T(128)S(1)}, s32[60,2]{0,1:T(2,128)S(1)}, s32[]{:T(128)}, /*index=5*/s32[40,5]{0,1...) while((s32[]{:T(128)}, ...), condition=%wide.region_1.2_spmd.clone.clone, body=%wide.region_0.1_spmd.clone.clone.sunk | while | flops 1352506368 | bytes 91372768 | solution.py:88
  43.9 4.9 %gather_fusion = bf16[50,2,128,128]{3,2,1,0:T(8,128)(2,1)} fusion(bf16[60,2,128,128]{3,2,1,0:T(8,128)(2,1)} %get-tuple-element.571, s32[1024]{0:T(1024)S(1)} %pad_clamp_fusion.6), kind=kCustom, calls=%fused_computation.2.clone.clone.1 | custom fusion | bytes 6553800 | tf_op jit(solution)/shard_map/while/body/eval_jaxpr/jit(_take)/gather | solution.py:64
  48.8 4.3 copy.98
  53.1 5.2 %fusion.101 = f32[10,5,2,128,128]{3,4,2,1,0:T(8,128)} fusion(bf16[10,5,2,128,128]{3,4,2,1,0:T(8,128)(2,1)S(1)} %copy.98, pred[10,5]{1,0:T(8,128)(4,1)S(1)} %get-tuple-element.531, bf16[40,5,128,128]{3,2,1,0:T(8,128)(2,1)} %get-tuple-element.572, s32[]{:T(128)S(6)} %select_n.363), kind=kOutput, calls=%fused_computation.14.clone.1 | convolution fusion | flops 421068800 | bytes 11468854 | tf_op jit(solution)/shard_map/while/body/eval_jaxpr/iakm,iaqmn->iaqkn/dot_general | solution.py:69
  58.3 10.1 %copy.99 = f32[10,5,2,128,128]{4,1,2,3,0:T(8,128)} copy(f32[10,5,2,128,128]{3,4,2,1,0:T(8,128)} %fusion.101) | data formatting | bytes 13107200 | tf_op jit(solution)/shard_map/while/body/eval_jaxpr/iakm,iaqmn->iaqkn/transpose | solution.py:69
  70.0 10.6 %fusion.103 = bf16[10,5,128,128,1]{3,1,2,0,4:T(8,128)(2,1)S(1)} fusion(f32[10,5,2,128,128]{4,1,2,3,0:T(8,128)} %copy.99, s32[10,5,2]{1,2,0:T(2,128)S(1)} %copy.102, s32[5]{0:T(128)S(1)} %iota_add_fusion.3), kind=kOutput, calls=%fused_computation.16.clone.1 | convolution fusion | flops 99123696 | bytes 8192420 | tf_op jit(solution)/shard_map/while/body/eval_jaxpr/iaqo,iaqkn->iokn/dot_general | solution.py:72
  80.6 3.8 convolution_bitcast_fusion.2
  84.4 11.5 %copy.103 = f32[10,2,5,128,128]{4,0,1,2,3:T(8,128)} copy(f32[10,2,5,128,128]{3,4,1,2,0:T(8,128)} %convolution_bitcast_fusion.2) | data formatting | bytes 13107200 | tf_op jit(solution)/shard_map/while/body/eval_jaxpr/ipmk,iomn->ipokn/transpose | solution.py:78
  96.1 12.4 %bitcast_dynamic-update-slice_fusion.2 = f32[4,3,7,128,128]{4,2,3,1,0:T(8,128)} fusion(f32[4,3,7,128,128]{4,2,3,1,0:T(8,128)} %get-tuple-element.550, s32[]{:T(128)} %get-tuple-element.549, f32[10,2,5,128,128]{4,0,1,2,3:T(8,128)} %copy.103, pred[10,2,5,7]{0,3,1,2:T(8,128)(4,1)S(1)} %iota_compare_fusion.6, pred[10,2,3]{0,1,2:T(4,128)(4,1)S(1)} %iota_compare_fusion.7), kind=kOutput, calls=%fused_computation.21.clone.1 | convolution fusion | flops 412878912 | bytes 12059896 | tf_op jit(solution)/shard_map/while/body/eval_jaxpr/ipots,ipokn->tskn/dot_general | solution.py:86
  110.2 4.9 %gather_fusion = bf16[50,2,128,128]{3,2,1,0:T(8,128)(2,1)} fusion(bf16[60,2,128,128]{3,2,1,0:T(8,128)(2,1)} %get-tuple-element.571, s32[1024]{0:T(1024)S(1)} %pad_clamp_fusion.6), kind=kCustom, calls=%fused_computation.2.clone.clone.1 | custom fusion | bytes 6553800 | tf_op jit(solution)/shard_map/while/body/eval_jaxpr/jit(_take)/gather | solution.py:64
  115.1 4.3 copy.98
  119.4 5.2 %fusion.101 = f32[10,5,2,128,128]{3,4,2,1,0:T(8,128)} fusion(bf16[10,5,2,128,128]{3,4,2,1,0:T(8,128)(2,1)S(1)} %copy.98, pred[10,5]{1,0:T(8,128)(4,1)S(1)} %get-tuple-element.531, bf16[40,5,128,128]{3,2,1,0:T(8,128)(2,1)} %get-tuple-element.572, s32[]{:T(128)S(6)} %select_n.363), kind=kOutput, calls=%fused_computation.14.clone.1 | convolution fusion | flops 421068800 | bytes 11468854 | tf_op jit(solution)/shard_map/while/body/eval_jaxpr/iakm,iaqmn->iaqkn/dot_general | solution.py:69
  124.6 10.1 %copy.99 = f32[10,5,2,128,128]{4,1,2,3,0:T(8,128)} copy(f32[10,5,2,128,128]{3,4,2,1,0:T(8,128)} %fusion.101) | data formatting | bytes 13107200 | tf_op jit(solution)/shard_map/while/body/eval_jaxpr/iakm,iaqmn->iaqkn/transpose | solution.py:69
  136.3 10.6 %fusion.103 = bf16[10,5,128,128,1]{3,1,2,0,4:T(8,128)(2,1)S(1)} fusion(f32[10,5,2,128,128]{4,1,2,3,0:T(8,128)} %copy.99, s32[10,5,2]{1,2,0:T(2,128)S(1)} %copy.102, s32[5]{0:T(128)S(1)} %iota_add_fusion.3), kind=kOutput, calls=%fused_computation.16.clone.1 | convolution fusion | flops 99123696 | bytes 8192420 | tf_op jit(solution)/shard_map/while/body/eval_jaxpr/iaqo,iaqkn->iokn/dot_general | solution.py:72
  147.0 3.8 convolution_bitcast_fusion.2
  150.7 11.5 %copy.103 = f32[10,2,5,128,128]{4,0,1,2,3:T(8,128)} copy(f32[10,2,5,128,128]{3,4,1,2,0:T(8,128)} %convolution_bitcast_fusion.2) | data formatting | bytes 13107200 | tf_op jit(solution)/shard_map/while/body/eval_jaxpr/ipmk,iomn->ipokn/transpose | solution.py:78
  162.4 12.4 %bitcast_dynamic-update-slice_fusion.2 = f32[4,3,7,128,128]{4,2,3,1,0:T(8,128)} fusion(f32[4,3,7,128,128]{4,2,3,1,0:T(8,128)} %get-tuple-element.550, s32[]{:T(128)} %get-tuple-element.549, f32[10,2,5,128,128]{4,0,1,2,3:T(8,128)} %copy.103, pred[10,2,5,7]{0,3,1,2:T(8,128)(4,1)S(1)} %iota_compare_fusion.6, pred[10,2,3]{0,1,2:T(4,128)(4,1)S(1)} %iota_compare_fusion.7), kind=kOutput, calls=%fused_computation.21.clone.1 | convolution fusion | flops 412878912 | bytes 12059896 | tf_op jit(solution)/shard_map/while/body/eval_jaxpr/ipots,ipokn->tskn/dot_general | solution.py:86
  176.5 4.9 %gather_fusion = bf16[50,2,128,128]{3,2,1,0:T(8,128)(2,1)} fusion(bf16[60,2,128,128]{3,2,1,0:T(8,128)(2,1)} %get-tuple-element.571, s32[1024]{0:T(1024)S(1)} %pad_clamp_fusion.6), kind=kCustom, calls=%fused_computation.2.clone.clone.1 | custom fusion | bytes 6553800 | tf_op jit(solution)/shard_map/while/body/eval_jaxpr/jit(_take)/gather | solution.py:64
  181.4 4.3 copy.98
  185.7 5.2 %fusion.101 = f32[10,5,2,128,128]{3,4,2,1,0:T(8,128)} fusion(bf16[10,5,2,128,128]{3,4,2,1,0:T(8,128)(2,1)S(1)} %copy.98, pred[10,5]{1,0:T(8,128)(4,1)S(1)} %get-tuple-element.531, bf16[40,5,128,128]{3,2,1,0:T(8,128)(2,1)} %get-tuple-element.572, s32[]{:T(128)S(6)} %select_n.363), kind=kOutput, calls=%fused_computation.14.clone.1 | convolution fusion | flops 421068800 | bytes 11468854 | tf_op jit(solution)/shard_map/while/body/eval_jaxpr/iakm,iaqmn->iaqkn/dot_general | solution.py:69
  190.9 10.1 %copy.99 = f32[10,5,2,128,128]{4,1,2,3,0:T(8,128)} copy(f32[10,5,2,128,128]{3,4,2,1,0:T(8,128)} %fusion.101) | data formatting | bytes 13107200 | tf_op jit(solution)/shard_map/while/body/eval_jaxpr/iakm,iaqmn->iaqkn/transpose | solution.py:69
  202.6 10.6 %fusion.103 = bf16[10,5,128,128,1]{3,1,2,0,4:T(8,128)(2,1)S(1)} fusion(f32[10,5,2,128,128]{4,1,2,3,0:T(8,128)} %copy.99, s32[10,5,2]{1,2,0:T(2,128)S(1)} %copy.102, s32[5]{0:T(128)S(1)} %iota_add_fusion.3), kind=kOutput, calls=%fused_computation.16.clone.1 | convolution fusion | flops 99123696 | bytes 8192420 | tf_op jit(solution)/shard_map/while/body/eval_jaxpr/iaqo,iaqkn->iokn/dot_general | solution.py:72
  213.3 3.8 convolution_bitcast_fusion.2
  217.0 11.5 %copy.103 = f32[10,2,5,128,128]{4,0,1,2,3:T(8,128)} copy(f32[10,2,5,128,128]{3,4,1,2,0:T(8,128)} %convolution_bitcast_fusion.2) | data formatting | bytes 13107200 | tf_op jit(solution)/shard_map/while/body/eval_jaxpr/ipmk,iomn->ipokn/transpose | solution.py:78
  228.7 12.4 %bitcast_dynamic-update-slice_fusion.2 = f32[4,3,7,128,128]{4,2,3,1,0:T(8,128)} fusion(f32[4,3,7,128,128]{4,2,3,1,0:T(8,128)} %get-tuple-element.550, s32[]{:T(128)} %get-tuple-element.549, f32[10,2,5,128,128]{4,0,1,2,3:T(8,128)} %copy.103, pred[10,2,5,7]{0,3,1,2:T(8,128)(4,1)S(1)} %iota_compare_fusion.6, pred[10,2,3]{0,1,2:T(4,128)(4,1)S(1)} %iota_compare_fusion.7), kind=kOutput, calls=%fused_computation.21.clone.1 | convolution fusion | flops 412878912 | bytes 12059896 | tf_op jit(solution)/shard_map/while/body/eval_jaxpr/ipots,ipokn->tskn/dot_general | solution.py:86
  242.8 4.9 %gather_fusion = bf16[50,2,128,128]{3,2,1,0:T(8,128)(2,1)} fusion(bf16[60,2,128,128]{3,2,1,0:T(8,128)(2,1)} %get-tuple-element.571, s32[1024]{0:T(1024)S(1)} %pad_clamp_fusion.6), kind=kCustom, calls=%fused_computation.2.clone.clone.1 | custom fusion | bytes 6553800 | tf_op jit(solution)/shard_map/while/body/eval_jaxpr/jit(_take)/gather | solution.py:64
  247.7 4.3 copy.98
  252.0 5.2 %fusion.101 = f32[10,5,2,128,128]{3,4,2,1,0:T(8,128)} fusion(bf16[10,5,2,128,128]{3,4,2,1,0:T(8,128)(2,1)S(1)} %copy.98, pred[10,5]{1,0:T(8,128)(4,1)S(1)} %get-tuple-element.531, bf16[40,5,128,128]{3,2,1,0:T(8,128)(2,1)} %get-tuple-element.572, s32[]{:T(128)S(6)} %select_n.363), kind=kOutput, calls=%fused_computation.14.clone.1 | convolution fusion | flops 421068800 | bytes 11468854 | tf_op jit(solution)/shard_map/while/body/eval_jaxpr/iakm,iaqmn->iaqkn/dot_general | solution.py:69
  257.2 10.1 %copy.99 = f32[10,5,2,128,128]{4,1,2,3,0:T(8,128)} copy(f32[10,5,2,128,128]{3,4,2,1,0:T(8,128)} %fusion.101) | data formatting | bytes 13107200 | tf_op jit(solution)/shard_map/while/body/eval_jaxpr/iakm,iaqmn->iaqkn/transpose | solution.py:69
  268.9 10.6 %fusion.103 = bf16[10,5,128,128,1]{3,1,2,0,4:T(8,128)(2,1)S(1)} fusion(f32[10,5,2,128,128]{4,1,2,3,0:T(8,128)} %copy.99, s32[10,5,2]{1,2,0:T(2,128)S(1)} %copy.102, s32[5]{0:T(128)S(1)} %iota_add_fusion.3), kind=kOutput, calls=%fused_computation.16.clone.1 | convolution fusion | flops 99123696 | bytes 8192420 | tf_op jit(solution)/shard_map/while/body/eval_jaxpr/iaqo,iaqkn->iokn/dot_general | solution.py:72
  279.5 3.8 convolution_bitcast_fusion.2
  283.3 11.5 %copy.103 = f32[10,2,5,128,128]{4,0,1,2,3:T(8,128)} copy(f32[10,2,5,128,128]{3,4,1,2,0:T(8,128)} %convolution_bitcast_fusion.2) | data formatting | bytes 13107200 | tf_op jit(solution)/shard_map/while/body/eval_jaxpr/ipmk,iomn->ipokn/transpose | solution.py:78
  295.0 12.4 %bitcast_dynamic-update-slice_fusion.2 = f32[4,3,7,128,128]{4,2,3,1,0:T(8,128)} fusion(f32[4,3,7,128,128]{4,2,3,1,0:T(8,128)} %get-tuple-element.550, s32[]{:T(128)} %get-tuple-element.549, f32[10,2,5,128,128]{4,0,1,2,3:T(8,128)} %copy.103, pred[10,2,5,7]{0,3,1,2:T(8,128)(4,1)S(1)} %iota_compare_fusion.6, pred[10,2,3]{0,1,2:T(4,128)(4,1)S(1)} %iota_compare_fusion.7), kind=kOutput, calls=%fused_computation.21.clone.1 | convolution fusion | flops 412878912 | bytes 12059896 | tf_op jit(solution)/shard_map/while/body/eval_jaxpr/ipots,ipokn->tskn/dot_general | solution.py:86
  313.3 17.3 %collective-permute-done.2 = f32[1,7,128,128]{3,1,2,0:T(8,128)S(1)} collective-permute-done((f32[1,7,128,128]{3,1,2,0:T(8,128)S(1)}, f32[1,7,128,128]{3,1,2,0:T(8,128)S(1)}, u32[]{:S(2)}, u32[]{:S(2)}) %collective-permute-start.2) | collective-permute-done | bytes 458784 | tf_op jit(solution)/shard_map/ppermute | solution.py:15
  332.6 9.9 %collective-permute-done.3 = f32[1,7,128,128]{3,1,2,0:T(8,128)S(1)} collective-permute-done((f32[1,7,128,128]{3,1,2,0:T(8,128)S(1)}, f32[1,7,128,128]{3,1,2,0:T(8,128)S(1)}, u32[]{:S(2)}, u32[]{:S(2)}) %collective-permute-start.3) | collective-permute-done | bytes 458784 | tf_op jit(solution)/shard_map/ppermute | solution.py:18
  342.6 3.4 fusion.42
  348.5 7.2 %all-to-all-start = ((f32[8,7,128,128]{3,2,1,0:T(8,128)}), f32[8,7,128,128]{3,2,1,0:T(8,128)}, u32[]{:S(2)}, u32[]{:S(2)}) async-start(f32[8,7,128,128]{3,2,1,0:T(8,128)} %copy.59), calls=%async_computation | async-start | bytes 7340032 | tf_op jit(solution)/shard_map/all_to_all | solution.py:101
  360.2 38.9 %all-to-all-done = f32[8,7,128,128]{3,2,1,0:T(8,128)} async-done(((f32[8,7,128,128]{3,2,1,0:T(8,128)}), f32[8,7,128,128]{3,2,1,0:T(8,128)}, u32[]{:S(2)}, u32[]{:S(2)}) %all-to-all-start) | async-done | bytes 3670048 | tf_op jit(solution)/shard_map/all_to_all | solution.py:101
  399.0 5.5 %fusion.48 = f32[8,1,128,1]{2,1,3,0:T(1,128)S(1)} fusion(f32[8,7,128,128]{3,2,1,0:T(8,128)} %all-to-all-done, f32[8,7,128,1]{2,1,0,3:T(8,128)S(1)} %select_bitcast_fusion.1), kind=kOutput, calls=%fused_computation.80 | convolution fusion | flops 11010048 | bytes 3702784 | tf_op jit(solution)/shard_map/gsmn,gsn->gm/dot_general | solution.py:127
  404.7 39.3 %all_to_all.27 = f32[256,8,128]{2,1,0:T(8,128)S(1)} all-to-all(f32[256,8,128]{2,1,0:T(8,128)S(1)} %stack.5), channel_id=1, replica_groups=mesh['grp'=8,'row'=32] {'grp','row'}, dimensions={0} | all-to-all | bytes 2097152 | tf_op jit(solution)/shard_map/all_to_all | solution.py:118
  444.6 5.6 %fusion.46 = f32[8,1,128,1]{2,1,3,0:T(1,128)S(1)} fusion(f32[8,7,128,128]{3,2,1,0:T(8,128)} %all-to-all-done, f32[8,7,128,1]{2,1,0,3:T(8,128)S(1)} %select_bitcast_fusion), kind=kOutput, calls=%fused_computation.78 | convolution fusion | flops 11010048 | bytes 3702784 | tf_op jit(solution)/shard_map/gsmn,gsn->gm/dot_general | solution.py:127
  450.8 4.3 copy.118
  (152 shorter events, 31.6 us)
Async XLA Ops:
  0.6 12.2 %copy-start = (f32[4,128]{1,0:T(4,128)S(1)}, f32[4,128]{1,0:T(4,128)}, u32[]{:S(2)}) copy-start(f32[4,128]{1,0:T(4,128)} %param.27) | copy-start | bytes 6148
  2.9 35.8 %collective-permute-start = (bf16[10,2,128,128]{3,2,1,0:T(8,128)(2,1)}, bf16[10,2,128,128]{3,2,1,0:T(8,128)(2,1)}, u32[]{:S(2)}, u32[]{:S(2)}) collective-permute-start(bf16[10,2,128,128]{3,2,1,0:T(8,128)(2,1)} %get-tuple-element.459), channel_id=1, source_target_pairs={{0,1},{1,2},{2,3},{3,4},{4,5},{5,6},{6,7},{7,8},{8,9},{9,10},{10,1... | collective-permute-start | bytes 1966088 | tf_op jit(solution)/shard_map/ppermute | solution.py:15
  4.9 33.7 %collective-permute-start.1 = (bf16[10,2,128,128]{3,2,1,0:T(8,128)(2,1)S(1)}, bf16[10,2,128,128]{3,2,1,0:T(8,128)(2,1)}, u32[]{:S(2)}, u32[]{:S(2)}) collective-permute-start(bf16[10,2,128,128]{3,2,1,0:T(8,128)(2,1)S(1)} %get-tuple-element.460), channel_id=1, source_target_pairs={{1,0},{2,1},{3,2},{4,3},{5,4},{6,5},{7,6},{8,7},{9,8},{10,9},{11,1... | collective-permute-start | bytes 1966088 | tf_op jit(solution)/shard_map/ppermute | solution.py:18
  13.7 14.2 %all-to-all-start.1 = ((f32[8,1,128]{2,1,0:T(1,128)}), f32[8,1,128]{2,1,0:T(1,128)S(1)}, u32[]{:S(2)}, u32[]{:S(2)}) async-start(f32[8,1,128]{2,1,0:T(1,128)} %bitcast.7), calls=%async_computation.1 | async-start | bytes 8192 | tf_op jit(solution)/shard_map/all_to_all | solution.py:102
  19.2 19.5 %copy-start.3 = (bf16[40,2,128,128]{3,2,1,0:T(8,128)(2,1)S(1)}, bf16[40,2,128,128]{3,2,1,0:T(8,128)(2,1)}, u32[]{:S(2)}) copy-start(bf16[40,2,128,128]{3,2,1,0:T(8,128)(2,1)} %param.25) | copy-start | bytes 7864324
  27.8 14.1 %copy-start.7 = (f32[8,1,128]{2,1,0:T(1,128)}, f32[8,1,128]{2,1,0:T(1,128)S(1)}, u32[]{:S(2)}) copy-start(f32[8,1,128]{2,1,0:T(1,128)S(1)} %all-to-all-done.1) | copy-start | bytes 12292
  28.9 319.6 %all-to-all-start.2 = ((f32[256,8,128]{2,1,0:T(8,128)}), f32[256,8,128]{2,1,0:T(8,128)}, u32[]{:S(2)}, u32[]{:S(2)}) async-start(f32[256,8,128]{2,1,0:T(8,128)} %stack.4), calls=%async_computation.2 | async-start | bytes 2097152 | tf_op jit(solution)/shard_map/all_to_all | solution.py:118
  38.6 3.3 copy-start.6
  70.0 10.6 %copy-start.4 = (bf16[40,2,128,128]{3,2,1,0:T(8,128)(2,1)S(1)}, bf16[40,2,128,128]{3,2,1,0:T(8,128)(2,1)}, u32[]{:S(2)}) copy-start(bf16[40,2,128,128]{3,2,1,0:T(8,128)(2,1)} %get-tuple-element.600) | copy-start | bytes 7864324 | tf_op jit(solution)/shard_map/while
  136.3 10.6 %copy-start.4 = (bf16[40,2,128,128]{3,2,1,0:T(8,128)(2,1)S(1)}, bf16[40,2,128,128]{3,2,1,0:T(8,128)(2,1)}, u32[]{:S(2)}) copy-start(bf16[40,2,128,128]{3,2,1,0:T(8,128)(2,1)} %get-tuple-element.600) | copy-start | bytes 7864324 | tf_op jit(solution)/shard_map/while
  202.6 10.6 %copy-start.4 = (bf16[40,2,128,128]{3,2,1,0:T(8,128)(2,1)S(1)}, bf16[40,2,128,128]{3,2,1,0:T(8,128)(2,1)}, u32[]{:S(2)}) copy-start(bf16[40,2,128,128]{3,2,1,0:T(8,128)(2,1)} %get-tuple-element.600) | copy-start | bytes 7864324 | tf_op jit(solution)/shard_map/while
  268.9 10.6 %copy-start.4 = (bf16[40,2,128,128]{3,2,1,0:T(8,128)(2,1)S(1)}, bf16[40,2,128,128]{3,2,1,0:T(8,128)(2,1)}, u32[]{:S(2)}) copy-start(bf16[40,2,128,128]{3,2,1,0:T(8,128)(2,1)} %get-tuple-element.600) | copy-start | bytes 7864324 | tf_op jit(solution)/shard_map/while
  307.4 3.4 copy-start.5
  311.6 19.1 %collective-permute-start.2 = (f32[1,7,128,128]{3,1,2,0:T(8,128)S(1)}, f32[1,7,128,128]{3,1,2,0:T(8,128)S(1)}, u32[]{:S(2)}, u32[]{:S(2)}) collective-permute-start(f32[1,7,128,128]{3,1,2,0:T(8,128)S(1)} %slice.195), channel_id=1, source_target_pairs={{0,1},{1,2},{2,3},{3,4},{4,5},{5,6},{6,7},{7,8},{8,9},{9,10},{10,1... | collective-permute-start | bytes 1376264 | tf_op jit(solution)/shard_map/ppermute | solution.py:15
  330.8 11.7 %collective-permute-start.3 = (f32[1,7,128,128]{3,1,2,0:T(8,128)S(1)}, f32[1,7,128,128]{3,1,2,0:T(8,128)S(1)}, u32[]{:S(2)}, u32[]{:S(2)}) collective-permute-start(f32[1,7,128,128]{3,1,2,0:T(8,128)S(1)} %get-tuple-element.457), channel_id=1, source_target_pairs={{1,0},{2,1},{3,2},{4,3},{5,4},{6,5},{7,6},{8,7},{9,8},{10,9},{11,1... | collective-permute-start | bytes 1376264 | tf_op jit(solution)/shard_map/ppermute | solution.py:18
  348.5 7.5 %copy-start.2 = (s32[1024]{0:T(1024)S(1)}, s32[1024]{0:T(1024)}, u32[]{:S(2)}) copy-start(s32[1024]{0:T(1024)} %param.26) | copy-start | bytes 12292
  348.5 50.5 %all-to-all-start = ((f32[8,7,128,128]{3,2,1,0:T(8,128)}), f32[8,7,128,128]{3,2,1,0:T(8,128)}, u32[]{:S(2)}, u32[]{:S(2)}) async-start(f32[8,7,128,128]{3,2,1,0:T(8,128)} %copy.59), calls=%async_computation | async-start | bytes 7340032 | tf_op jit(solution)/shard_map/all_to_all | solution.py:101
  357.2 47.4 %copy-start.8 = (f32[8,1,128]{2,1,0:T(1,128)S(1)}, f32[8,1,128]{2,1,0:T(1,128)}, u32[]{:S(2)}) copy-start(f32[8,1,128]{2,1,0:T(1,128)} %copy-done.7) | copy-start | bytes 12292
  404.6 45.6 %copy-start.9 = (f32[8,128]{1,0:T(8,128)}, f32[8,128]{1,0:T(8,128)S(1)}, u32[]{:S(2)}) copy-start(f32[8,128]{1,0:T(8,128)S(1)} %fusion.50) | copy-start | bytes 12292
  450.2 4.9 %copy-start.1 = (f32[4,128]{1,0:T(4,128)S(1)}, f32[4,128]{1,0:T(4,128)}, u32[]{:S(2)}) copy-start(f32[4,128]{1,0:T(4,128)} %param.27) | copy-start | bytes 6148
